TPU v7x, 256 devices: a whole 4x4x8 slice. The times are simulated.
256 devices in a mesh: rep: 2 (over core), req: 32 (over y, z), tp: 4 (over x).
Axes of the slice: x: 4, y: 4, z: 8, core: 2. Of those that a mesh axis runs over, the one named last changes fastest.
Arguments:
- hidden: bfloat16 [1024, 1536], P(('rep', 'req'), 'tp'), may hold values from -6 to 6
- lengths: int32 [2, 512], P(None, 'req'), may hold values from 16 to 1024, as said below
- migrate: int32 [32], P('req'), may hold values from 0 to 15
- kv_cache: bfloat16 [1024, 1024, 8, 128], P(('rep', 'req'), None, 'tp'), may hold values from -250 to 250
- attn_gain: float32 [1536], replicated, may hold values from 0.1 to 1.9
- moe_gain: float32 [1536], replicated, may hold values from 0.1 to 1.9
- w_query: bfloat16 [1536, 1536], P(None, 'tp'), may hold values from -0.15625 to 0.15625
- key_value_weight: bfloat16 [1536, 1024], P(None, 'tp'), may hold values from -0.15625 to 0.15625
- output_weight: bfloat16 [1536, 1536], P('tp'), may hold values from -0.25 to 0.25
- w_gateup: bfloat16 [64, 1536, 2, 512], P(('rep', 'req'), None, None, 'tp'), may hold values from -0.15625 to 0.15625
- w_down: bfloat16 [64, 512, 1536], P(('rep', 'req'), 'tp'), may hold values from -0.25 to 0.25
- expert_ids: int32 [1024, 8], P(('rep', 'req')), may hold values from 0 to 63, all different within a row; in each aligned block of 16 rows (0 to 15, 16 to 31, ...) at most 6 rows name the same one
- expert_gates: float32 [1024, 8], P(('rep', 'req')), may hold values from 0.1 to 0.4
Outputs:
- layer_out: bfloat16 [1024, 1536], P(('rep', 'req'), 'tp')
Inputs may be any that keep to these rules, and one draw needn't show every extreme that they name: A request attends to its first lengths positions and to its own new key. `expert_ids`: each row names 8 distinct experts; among the rows of one device (an aligned block of 16 rows) no expert is named more than 6 times, and in some blocks one expert is named exactly 6 times.
All inputs are finite; a program needn't handle non-finite values.
Results may differ from a plain program's by a relative error of at most 0.015.
Values may be sent and summed in bfloat16 or wider, within the bound.
A program may use at most 64 MiB of HBM per device.

v0:
```python
import jax
import jax.numpy as jnp
from jax import lax
from jax.sharding import PartitionSpec as P

HEAD_SIZE = 64
epsilon = 1e-06
rope_base = 10000.0
masked_score = -1e30


def swapped(value, axis, apart):
    return lax.ppermute(value, axis, [(i, i ^ 1 << apart) for i in range(lax.axis_size(axis))])


def rms_norm(values, gain):
    mean_square = jnp.mean(values * values, axis=-1, keepdims=True)
    return values * lax.rsqrt(mean_square + epsilon) * gain


def apply_rotation(values, position):
    half_width = values.shape[-1] // 2
    inv_freq = rope_base ** (-jnp.arange(half_width, dtype=jnp.float32) * 2.0 / values.shape[-1])
    angles = position.astype(jnp.float32)[:, None, None] * inv_freq
    cosine = jnp.cos(angles)
    sine_part = jnp.sin(angles)
    first_half = values[..., :half_width]
    second_half = values[..., half_width:]
    return jnp.concatenate(
        [
            first_half * cosine - second_half * sine_part,
            second_half * cosine + first_half * sine_part,
        ],
        axis=-1,
    )


def attention(
    token_part, kv_rows, request_extent, attn_gain, w_query, key_value_weight, output_weight
):
    tokens = lax.all_gather(token_part, "tp", axis=1, tiled=True)
    row_count = tokens.shape[0]
    head_dim = HEAD_SIZE
    local_kv = kv_rows.shape[2]
    local_query = w_query.shape[1] // head_dim
    group_size = local_query // local_kv
    normalized_input = rms_norm(tokens.astype(jnp.float32), attn_gain).astype(jnp.bfloat16)
    query_vectors = jnp.dot(normalized_input, w_query, preferred_element_type=jnp.float32).reshape(
        row_count, local_query, head_dim
    )
    key_value_rows = jnp.dot(
        normalized_input, key_value_weight, preferred_element_type=jnp.float32
    ).reshape(row_count, local_kv, 2 * head_dim)
    query_vectors = (
        apply_rotation(query_vectors, request_extent)
        .astype(jnp.bfloat16)
        .reshape(row_count, local_kv, group_size, head_dim)
    )
    key_new = apply_rotation(key_value_rows[..., :head_dim], request_extent).astype(jnp.bfloat16)
    value_new = key_value_rows[..., head_dim:].astype(jnp.bfloat16)
    score_scale = head_dim ** (-0.5)
    cache_keys = kv_rows[..., :head_dim]
    cache_values = kv_rows[..., head_dim:]
    scores = (
        jnp.einsum("rhgd,rthd->rhgt", query_vectors, cache_keys, preferred_element_type=jnp.float32)
        * score_scale
    )
    own_score = (
        jnp.einsum("rhgd,rhd->rhg", query_vectors, key_new, preferred_element_type=jnp.float32)
        * score_scale
    )
    positions = jnp.arange(kv_rows.shape[1], dtype=jnp.int32)
    visible = positions[None, None, None, :] < request_extent[:, None, None, None]
    scores = jnp.where(visible, scores, masked_score)
    row_peak = jnp.maximum(jnp.max(scores, axis=-1), own_score)
    cache_prob = jnp.exp(scores - row_peak[..., None])
    own_prob = jnp.exp(own_score - row_peak)
    denominator = jnp.sum(cache_prob, axis=-1) + own_prob
    cache_weight = (cache_prob / denominator[..., None]).astype(jnp.bfloat16)
    own_weight = (own_prob / denominator).astype(jnp.bfloat16)
    mixture = jnp.einsum(
        "rhgt,rthd->rhgd", cache_weight, cache_values, preferred_element_type=jnp.float32
    )
    mixture = (
        mixture
        + own_weight.astype(jnp.float32)[..., None] * value_new.astype(jnp.float32)[:, :, None, :]
    )
    context = mixture.reshape(row_count, local_query * head_dim).astype(jnp.bfloat16)
    partial_out = jnp.dot(context, output_weight, preferred_element_type=jnp.float32)
    return tokens.astype(jnp.float32) + lax.psum(partial_out.astype(jnp.bfloat16), "tp").astype(
        jnp.float32
    )


def shards(
    hidden,
    lengths,
    migrate,
    kv_cache,
    attn_gain,
    moe_gain,
    w_query,
    key_value_weight,
    output_weight,
    w_gateup,
    w_down,
    expert_ids,
    expert_gates,
):
    row_count = hidden.shape[0]
    replica = lax.axis_index("rep")
    slot_index = jnp.arange(row_count, dtype=jnp.int32)
    chosen_slot = migrate[0]
    is_moved = slot_index == chosen_slot
    own_span = lax.dynamic_index_in_dim(lengths, replica, 0, keepdims=False)
    other_span = lax.dynamic_index_in_dim(lengths, 1 - replica, 0, keepdims=False)
    picked_cache = lax.dynamic_slice_in_dim(kv_cache, chosen_slot, 1, 0)
    picked_row = lax.dynamic_slice_in_dim(hidden, chosen_slot, 1, 0)
    cache_width = picked_cache.size
    packed = jnp.concatenate([picked_cache.reshape(1, cache_width), picked_row], axis=1)
    arrived = swapped(packed, "rep", 0)
    moved_cache = arrived[:, :cache_width].reshape(picked_cache.shape)
    moved_row = arrived[:, cache_width:]
    served_cache = lax.dynamic_update_slice_in_dim(kv_cache, moved_cache, chosen_slot, 0)
    served_rows = lax.dynamic_update_slice_in_dim(hidden, moved_row, chosen_slot, 0)
    request_extent = jnp.where(is_moved, other_span, own_span)
    residual = attention(
        served_rows,
        served_cache,
        request_extent,
        attn_gain,
        w_query,
        key_value_weight,
        output_weight,
    )
    full_width = moe_gain.shape[0]
    quarter = full_width // lax.axis_size("tp")
    expert_in = rms_norm(residual, moe_gain).astype(jnp.bfloat16)
    own_residual = lax.dynamic_slice_in_dim(residual, lax.axis_index("tp") * quarter, quarter, 1)
    expert_count = lax.axis_size("rep") * lax.axis_size("req")
    top_count = expert_ids.shape[1]
    capacity = min(row_count, max(3, 3 * row_count * top_count // expert_count))
    flat_ids = expert_ids.reshape(-1)
    matches = (flat_ids[:, None] == jnp.arange(expert_count, dtype=jnp.int32)[None, :]).astype(
        jnp.int32
    )
    slot_rank = jnp.sum((jnp.cumsum(matches, axis=0) - matches) * matches, axis=1)
    slot_target = flat_ids * capacity + slot_rank
    slot_table = (
        slot_target[:, None] == jnp.arange(expert_count * capacity, dtype=jnp.int32)[None, :]
    ).astype(jnp.float32)
    route_table = slot_table.reshape(row_count, top_count, -1).sum(axis=1)
    gate_table = (
        (slot_table * expert_gates.reshape(-1, 1)).reshape(row_count, top_count, -1).sum(axis=1)
    )
    outbound = jnp.einsum(
        "rs,rd->sd", route_table.astype(jnp.bfloat16), expert_in, preferred_element_type=jnp.float32
    ).astype(jnp.bfloat16)
    outbound = outbound.reshape(expert_count, capacity, -1)
    gate_up = w_gateup[0].reshape(w_gateup.shape[1], -1)
    down_rows = w_down[0]
    arrived_rows = lax.all_to_all(outbound, ("rep", "req"), split_axis=0, concat_axis=0, tiled=True)
    model_width = arrived_rows.shape[2]
    flattened = arrived_rows.reshape(-1, model_width)
    projected = jnp.dot(flattened, gate_up, preferred_element_type=jnp.float32)
    split_at = projected.shape[1] // 2
    activation = (jax.nn.silu(projected[:, :split_at]) * projected[:, split_at:]).astype(
        jnp.bfloat16
    )
    expert_part = jnp.dot(activation, down_rows, preferred_element_type=jnp.float32)
    expert_part = expert_part.reshape(arrived_rows.shape[0], arrived_rows.shape[1], model_width)
    returned = lax.all_to_all(
        expert_part.astype(jnp.bfloat16), ("rep", "req"), split_axis=0, concat_axis=0, tiled=True
    ).astype(expert_part.dtype)
    returned_rows = returned.reshape(expert_count * capacity, -1)
    combined = jnp.dot(
        gate_table,
        returned_rows,
        precision=lax.Precision.HIGHEST,
        preferred_element_type=jnp.float32,
    )
    expert_mix = lax.psum_scatter(
        combined.astype(jnp.bfloat16), "tp", scatter_dimension=1, tiled=True
    ).astype(jnp.float32)
    return (own_residual + expert_mix).astype(jnp.bfloat16)


def solution(mesh):
    placed = (
        P(("rep", "req"), "tp"),
        P(None, "req"),
        P("req"),
        P(("rep", "req"), None, "tp", None),
        P(),
        P(),
        P(None, "tp"),
        P(None, "tp"),
        P("tp", None),
        P(("rep", "req"), None, None, "tp"),
        P(("rep", "req"), "tp", None),
        P(("rep", "req"), None),
        P(("rep", "req"), None),
    )
    return jax.shard_map(
        shards, mesh=mesh, in_specs=placed, out_specs=P(("rep", "req"), "tp"), check_vma=False
    )
```

profile of v0, /device:TPU:8, one launch (start us, length us, event | category | flops | bytes accessed | tf_op | source)
XLA Modules:
  0.0 226.3 jit_solution(14845780851035790938)
XLA Ops:
  6.5 0.8 copy.69
  8.0 1.4 constant_dynamic-slice_fusion.3
  9.6 4.4 %pad_maximum_fusion = bf16[1,262528]{1,0:T(2,128)(2,1)S(1)} fusion(bf16[1,384]{1,0:T(2,128)(2,1)S(1)} %constant_dynamic-slice_fusion.2, bf16[1,262144]{1,0:T(2,128)(2,1)S(1)} %reshape.200), kind=kLoop, calls=%fused_computation.12 | loop fusion | flops 1050112 | bytes 1050112 | tf_op jit(solution)/shard_map/concatenate | solution.py:120
  14.2 21.2 %copy.45 = bf16[16,1024,2,128]{1,3,2,0:T(8,128)(2,1)} copy(bf16[16,1024,2,128]{3,2,1,0:T(2,128)(2,1)} %param.16) | data formatting | bytes 16777216 | tf_op args[3]
  36.1 0.2 convert_reduce_fusion
  36.6 1.0 copy-done.2
  37.7 12.2 %all_gather.3 = bf16[16,1536]{1,0:T(8,128)(2,1)S(1)} all-gather(bf16[16,384]{1,0:T(8,128)(2,1)S(1)} %dynamic_update_slice.6), channel_id=1, replica_groups=mesh['rep'=2,'req'=32,'tp'=4] {'tp'}, dimensions={1}, use_global_device_ids=true | all-gather | bytes 61440 | tf_op jit(solution)/shard_map/all_gather | solution.py:41
  49.9 9.9 %slice_reduce_fusion = bf16[262144]{0:T(1024)(128)(2,1)S(1)} fusion(bf16[1,262528]{1,0:T(2,128)(2,1)} %copy-done.2), kind=kLoop, calls=%fused_computation.13 | loop fusion | bytes 1048576 | tf_op jit(solution)/shard_map/slice | solution.py:122
  59.8 0.4 copy.46
  60.4 0.3 fusion.36
  60.8 1.4 fusion.34
  62.5 0.9 constant_dynamic-update-slice_fusion
  63.5 0.2 fusion.31
  63.7 3.0 %fusion.44 = (f32[16,2,3]{2,1,0:T(2,128)S(1)}, f32[16,2,3,1024]{3,2,1,0:T(4,128)S(1)}) fusion(bf16[16,1024,2,128]{1,3,2,0:T(8,128)(2,1)} %constant_dynamic-update-slice_fusion, bf16[16,2,3,32]{3,2,1,0:T(4,128)(2,1)S(1)} %copy.44, bf16[16,2,3,32]{3,2,1,0:T(4,128)(2,1)S(1)} %copy.43, pred[16,1024]{1,0:T(8,128)(4,1)S(1)} %iota_compare_fusion.2), kind=kOutput, calls=%fused_computation.77 | convolution fusion | flops 12902304 | bytes 4616576 | tf_op jit(solution)/shard_map/rhgd,rthd->rhgt/dot_general | solution.py:65
  66.8 0.3 fusion.19
  67.2 3.5 %fusion.13 = bf16[16,2,3,64]{3,2,1,0:T(4,128)(2,1)S(1)} fusion(bf16[16,1024,2,128]{1,3,2,0:T(8,128)(2,1)} %constant_dynamic-update-slice_fusion, f32[16,2,3,1024]{3,2,1,0:T(4,128)S(1)} %get-tuple-element.20, f32[16,2,3]{2,1,0:T(2,128)S(1)} %get-tuple-element.14, f32[16,2,3]{2,1,0:T(2,128)S(1)} %multiply_maximum_fusion, f32[16,2,64]{2,1,0:T(2,128)S(1)} %fusion.38, ...), kind=kOutput, calls=%fused_computation.11 | convolution fusion | flops 12896256 | bytes 4609152 | tf_op jit(solution)/shard_map/rhgt,rthd->rhgd/dot_general | solution.py:81
  70.7 0.3 convolution_convert_fusion.3
  71.0 17.0 %psum.7 = bf16[16,1536]{1,0:T(8,128)(2,1)S(1)} all-reduce(bf16[16,1536]{1,0:T(8,128)(2,1)S(1)} %convolution_convert_fusion.3), channel_id=1, replica_groups=mesh['rep'=2,'req'=32,'tp'=4] {'tp'}, use_global_device_ids=true, to_apply=%region_3.4 | all-reduce | flops 24576 | bytes 98304 | tf_op jit(solution)/shard_map/psum | solution.py:90
  88.2 1.5 convolution_convert_fusion
  89.7 2.2 reshape.204
  91.9 51.9 %all_to_all.10 = bf16[64,6,1536]{2,1,0:T(8,128)(2,1)} all-to-all(bf16[64,6,1536]{2,1,0:T(8,128)(2,1)S(1)} %reshape.204), channel_id=1, replica_groups=mesh['rep'=2,'req'=32,'tp'=4] {'rep','req'}, dimensions={0} | all-to-all | bytes 2359296 | tf_op jit(solution)/shard_map/all_to_all | solution.py:162
  143.8 2.3 %reshape.205 = bf16[384,1536]{1,0:T(8,128)(2,1)S(1)} reshape(bf16[64,6,1536]{2,1,0:T(8,128)(2,1)} %all_to_all.10) | data formatting | bytes 2359296 | tf_op jit(solution)/shard_map/reshape | solution.py:164
  146.1 1.7 fusion.16
  147.9 0.4 convolution_convert_fusion.1
  148.4 0.7 copy.51
  149.0 45.9 %all_to_all.11 = bf16[64,6,1536]{2,1,0:T(8,128)(2,1)S(1)} all-to-all(bf16[64,6,1536]{2,1,0:T(8,128)(2,1)S(1)} %copy.51), channel_id=1, replica_groups=mesh['rep'=2,'req'=32,'tp'=4] {'rep','req'}, dimensions={0} | all-to-all | bytes 2359296 | tf_op jit(solution)/shard_map/all_to_all | solution.py:172
  195.0 1.2 reshape.206
  196.2 1.8 convolution_convert_fusion.2
  198.0 0.9 copy.54
  199.0 18.9 %reduce-scatter.4.cloned.1.call-done = bf16[384,16]{1,0:T(8,128)(2,1)} async-done(((bf16[1536,16]{1,0:T(8,128)(2,1)}), bf16[384,16]{1,0:T(8,128)(2,1)}) %reduce-scatter.4.cloned.1.call-update) | async-done | bytes 12304
  217.9 1.0 copy.55
  218.9 0.6 add_convert_fusion.1
  (56 shorter events, 2.4 us)
Async XLA Ops:
  6.5 64.2 %copy-start = (bf16[384,1536]{1,0:T(8,128)(2,1)S(1)}, bf16[384,1536]{1,0:T(8,128)(2,1)}, u32[]{:S(2)}) copy-start(bf16[384,1536]{1,0:T(8,128)(2,1)} %param.21) | copy-start | bytes 3538948
  6.5 211.4 %reduce-scatter.4.cloned.1.call-start = ((), (), s32[]{:S(2)}) async-start(), calls=%async_computation.3 | async-start | bytes 491520
  14.0 21.3 %copy-start.6 = (s32[16,8]{0,1:T(8,128)S(1)}, s32[16,8]{0,1:T(8,128)}, u32[]{:S(2)}) copy-start(s32[16,8]{0,1:T(8,128)} %param.24) | copy-start | bytes 1540
  14.1 22.0 %copy-start.7 = (f32[16,8]{0,1:T(8,128)S(1)}, f32[16,8]{0,1:T(8,128)}, u32[]{:S(2)}) copy-start(f32[16,8]{0,1:T(8,128)} %param.25) | copy-start | bytes 1540
  14.1 22.3 %copy-start.8 = (s32[2,16]{1,0:T(2,128)S(1)}, s32[2,16]{1,0:T(2,128)}, u32[]{:S(2)}) copy-start(s32[2,16]{1,0:T(2,128)} %param.14) | copy-start | bytes 388
  14.1 22.5 %collective-permute-start = (bf16[1,262528]{1,0:T(2,128)(2,1)S(1)}, bf16[1,262528]{1,0:T(2,128)(2,1)S(1)}, u32[]{:S(2)}, u32[]{:S(2)}) collective-permute-start(bf16[1,262528]{1,0:T(2,128)(2,1)S(1)} %pad_maximum_fusion), channel_id=1, source_target_pairs={{0,128},{128,0},{1,129},{129,1},{2,130},{130,2},{3,131},{131,3},{4... | collective-permute-start | bytes 1575176 | tf_op jit(solution)/shard_map/ppermute | solution.py:13
  36.6 1.1 copy-start.2
  49.9 10.4 %copy-start.1 = (bf16[1536,384]{1,0:T(8,128)(2,1)S(1)}, bf16[1536,384]{1,0:T(8,128)(2,1)}, u32[]{:S(2)}) copy-start(bf16[1536,384]{1,0:T(8,128)(2,1)} %param.19) | copy-start | bytes 3538948
  49.9 10.4 %copy-start.4 = (f32[1536]{0:T(1024)S(1)}, f32[1536]{0:T(1024)}, u32[]{:S(2)}) copy-start(f32[1536]{0:T(1024)} %param.17) | copy-start | bytes 18436
  70.6 17.6 %copy-start.5 = (f32[1536]{0:T(1024)S(1)}, f32[1536]{0:T(1024)}, u32[]{:S(2)}) copy-start(f32[1536]{0:T(1024)} %param.18) | copy-start | bytes 18436
  146.1 1.8 copy-start.3
Sparse Core Ops, SparseCore 0:
  199.1 18.7 reduce-scatter.3
where the time goes:
time: 227 us; the launch traced here: 226 us
  blocking collectives  127 us (56%)
  local copies, waits for them, and re-layouts  44.7 us (20%)
  waiting for transfers between devices  18.9 us (8%)
  between operations  14.4 us (6%)
  matrix products  14.1 us (6%)
  other arithmetic  6.97 us (3%)
    all_to_all x1, blocking collectives, shards(): lax.all_to_all(outbound, ('rep', 'req'), split_axis=0, concat_axis=0, til...  51.9 us
    all_to_all x1, blocking collectives, shards(): lax.all_to_all(expert_part.astype(jnp.bfloat16), ('rep', 'req'), split_ax...  45.9 us
    unnamed x24, local copies, waits for them, and re-layouts  25.1 us
    unnamed x2, waiting for transfers between devices  18.9 us
    psum x1, blocking collectives, attention(): lax.psum(partial_out.astype(jnp.bfloat16), 'tp').astype(jnp.float32)  17 us
    all_gather x1, blocking collectives, attention(): tokens = lax.all_gather(token_part, 'tp', axis=1, tiled=True)  12.2 us
    slice x1, local copies, waits for them, and re-layouts, shards(): moved_cache = arrived[:, :cache_width].reshape(picked_cache.shape)  9.86 us
  transfers between devices with their start and end apart: 2, of which 1 were waited for; matrix products, arithmetic and copies ran while one was open for 10% of the time, Pallas kernels for 0%

commit v1 on v0

--- a/solution.py
+++ b/solution.py
@@ -38,7 +38,22 @@
 def attention(
     token_part, kv_rows, request_extent, attn_gain, w_query, key_value_weight, output_weight
 ):
-    tokens = lax.all_gather(token_part, "tp", axis=1, tiled=True)
+    ways, here, step = (lax.axis_size("tp"), lax.axis_index("tp"), token_part.shape[1])
+    shape = [n * ways if d == 1 else n for d, n in enumerate(token_part.shape)]
+    tokens = lax.dynamic_update_slice_in_dim(
+        jnp.zeros(shape, token_part.dtype), token_part, here * step, axis=1
+    )
+    going_up = going_down = token_part
+    for far in range(1, ways // 2 + 1):
+        going_up = lax.ppermute(going_up, "tp", [(d, (d + 1) % ways) for d in range(ways)])
+        tokens = lax.dynamic_update_slice_in_dim(
+            tokens, going_up, (here - far) % ways * step, axis=1
+        )
+        if 2 * far < ways:
+            going_down = lax.ppermute(going_down, "tp", [(d, (d - 1) % ways) for d in range(ways)])
+            tokens = lax.dynamic_update_slice_in_dim(
+                tokens, going_down, (here + far) % ways * step, axis=1
+            )
     row_count = tokens.shape[0]
     head_dim = HEAD_SIZE
     local_kv = kv_rows.shape[2]

time: 227 us -> 219 us (0.965)
  blocking collectives: 127 us -> 113 us
  waiting for transfers between devices: 18.9 us -> 23.8 us
  starting transfers between devices: 0.09 us -> 3.86 us
    all_gather x1 -> x0, blocking collectives: 12.2 us -> none  [attention(): tokens = lax.all_gather(token_part, 'tp', axis=1, tiled=True)]
    ppermute x0 -> x3, waiting for transfers between devices: none -> 4.61 us  [the longest x2 4.61 us: attention(): lax.ppermute(going_up, 'tp', [(d, (d + 1) % ways) for d in range(ways)])]
    ppermute x0 -> x3, starting transfers between devices: none -> 3.85 us  [the longest x2 2.11 us: attention(): lax.ppermute(going_up, 'tp', [(d, (d + 1) % ways) for d in range(ways)])]
  transfers between devices with their start and end apart: 2 -> 5, of which waited for: 1 -> 2; matrix products, arithmetic and copies ran while one was open for 10% -> 15% of each run, Pallas kernels for 0% -> 0%
where the time goes in v1:
time: 219 us; the launch traced here: 218 us
  blocking collectives  113 us (52%)
  local copies, waits for them, and re-layouts  42.6 us (19%)
  waiting for transfers between devices  23.8 us (11%)
  between operations  14.4 us (7%)
  matrix products  13 us (6%)
  other arithmetic  7.74 us (4%)
  starting transfers between devices  3.86 us (2%)
    all_to_all x1, blocking collectives, shards(): lax.all_to_all(outbound, ('rep', 'req'), split_axis=0, concat_axis=0, til...  51.9 us
    all_to_all x1, blocking collectives, shards(): lax.all_to_all(expert_part.astype(jnp.bfloat16), ('rep', 'req'), split_ax...  45.9 us
    unnamed x24, local copies, waits for them, and re-layouts  24.1 us
    unnamed x2, waiting for transfers between devices  19.2 us
    psum x1, blocking collectives, attention(): lax.psum(partial_out.astype(jnp.bfloat16), 'tp').astype(jnp.float32)  15 us
    slice x1, local copies, waits for them, and re-layouts, shards(): moved_cache = arrived[:, :cache_width].reshape(picked_cache.shape)  8.75 us
    concatenate x1, other arithmetic, shards(): jnp.concatenate([picked_cache.reshape(1, cache_width), picked_row], axis=1)  5.18 us
    ppermute x2, waiting for transfers between devices, attention(): lax.ppermute(going_up, 'tp', [(d, (d + 1) % ways) for d in range(ways)])  4.61 us
  transfers between devices with their start and end apart: 5, of which 2 were waited for; matrix products, arithmetic and copies ran while one was open for 15% of the time, Pallas kernels for 0%

profile of v1, /device:TPU:8, one launch (start us, length us, event | category | flops | bytes accessed | tf_op | source)
XLA Modules:
  0.0 218.2 jit_solution(18003673097740814038)
XLA Ops:
  6.5 0.8 copy.73
  8.0 1.4 constant_dynamic-slice_fusion.3
  9.6 5.2 %pad_maximum_fusion = bf16[1,262528]{1,0:T(2,128)(2,1)} fusion(bf16[1,384]{1,0:T(2,128)(2,1)S(1)} %constant_dynamic-slice_fusion.2, bf16[1,262144]{1,0:T(2,128)(2,1)S(1)} %reshape.200), kind=kLoop, calls=%fused_computation.12 | loop fusion | flops 1050112 | bytes 1050112 | tf_op jit(solution)/shard_map/concatenate | solution.py:135
  14.8 21.2 %copy.45 = bf16[16,1024,2,128]{1,3,2,0:T(8,128)(2,1)} copy(bf16[16,1024,2,128]{3,2,1,0:T(2,128)(2,1)} %param.16) | data formatting | bytes 16777216 | tf_op args[3]
  37.3 1.6 collective-permute-start.1
  38.9 1.7 collective-permute-start.2
  40.6 8.8 %slice_reduce_fusion = bf16[262144]{0:T(1024)(128)(2,1)S(1)} fusion(bf16[1,262528]{1,0:T(2,128)(2,1)S(1)} %collective-permute-done), kind=kLoop, calls=%fused_computation.13 | loop fusion | bytes 1048576 | tf_op jit(solution)/shard_map/slice | solution.py:137
  49.4 0.4 copy.46
  49.9 0.9 constant_dynamic-update-slice_fusion
  50.8 0.5 collective-permute-start.3
  51.3 4.6 %collective-permute-done.3 = bf16[16,384]{1,0:T(8,128)(2,1)S(1)} collective-permute-done((bf16[16,384]{1,0:T(8,128)(2,1)S(1)}, bf16[16,384]{1,0:T(8,128)(2,1)S(1)}, u32[]{:S(2)}, u32[]{:S(2)}) %collective-permute-start.3) | collective-permute-done | bytes 12320 | tf_op jit(solution)/shard_map/ppermute | solution.py:48
  56.1 0.3 fusion.36
  56.5 0.3 fusion.34
  57.4 3.0 %fusion.44 = (f32[16,2,3]{2,1,0:T(2,128)S(1)}, f32[16,2,3,1024]{3,2,1,0:T(4,128)S(1)}) fusion(bf16[16,1024,2,128]{1,3,2,0:T(8,128)(2,1)} %constant_dynamic-update-slice_fusion, bf16[16,2,3,32]{3,2,1,0:T(4,128)(2,1)S(1)} %copy.44, bf16[16,2,3,32]{3,2,1,0:T(4,128)(2,1)S(1)} %copy.43, pred[16,1024]{1,0:T(8,128)(4,1)S(1)} %iota_compare_fusion.2), kind=kOutput, calls=%fused_computation.81 | convolution fusion | flops 12902304 | bytes 4616576 | tf_op jit(solution)/shard_map/rhgd,rthd->rhgt/dot_general | solution.py:80
  60.5 0.3 fusion.19
  60.9 3.5 %fusion.13 = bf16[16,2,3,64]{3,2,1,0:T(4,128)(2,1)S(1)} fusion(bf16[16,1024,2,128]{1,3,2,0:T(8,128)(2,1)} %constant_dynamic-update-slice_fusion, f32[16,2,3,1024]{3,2,1,0:T(4,128)S(1)} %get-tuple-element.20, f32[16,2,3]{2,1,0:T(2,128)S(1)} %get-tuple-element.14, f32[16,2,3]{2,1,0:T(2,128)S(1)} %multiply_maximum_fusion, f32[16,2,64]{2,1,0:T(2,128)S(1)} %fusion.38, ...), kind=kOutput, calls=%fused_computation.11 | convolution fusion | flops 12896256 | bytes 4609152 | tf_op jit(solution)/shard_map/rhgt,rthd->rhgd/dot_general | solution.py:96
  64.4 0.3 convolution_convert_fusion.3
  64.7 15.0 %psum.7 = bf16[16,1536]{1,0:T(8,128)(2,1)S(1)} all-reduce(bf16[16,1536]{1,0:T(8,128)(2,1)S(1)} %convolution_convert_fusion.3), channel_id=1, replica_groups=mesh['rep'=2,'req'=32,'tp'=4] {'tp'}, use_global_device_ids=true, to_apply=%region_3.4 | all-reduce | flops 24576 | bytes 98304 | tf_op jit(solution)/shard_map/psum | solution.py:105
  79.8 1.5 convolution_convert_fusion
  81.3 2.2 %reshape.204 = bf16[64,6,1536]{2,1,0:T(8,128)(2,1)S(1)} reshape(bf16[384,1536]{1,0:T(8,128)(2,1)} %convolution_convert_fusion) | data formatting | bytes 2359296 | tf_op jit(solution)/shard_map/reshape | solution.py:174
  83.6 51.9 %all_to_all.10 = bf16[64,6,1536]{2,1,0:T(8,128)(2,1)} all-to-all(bf16[64,6,1536]{2,1,0:T(8,128)(2,1)S(1)} %reshape.204), channel_id=1, replica_groups=mesh['rep'=2,'req'=32,'tp'=4] {'rep','req'}, dimensions={0} | all-to-all | bytes 2359296 | tf_op jit(solution)/shard_map/all_to_all | solution.py:177
  135.4 2.3 %reshape.205 = bf16[384,1536]{1,0:T(8,128)(2,1)S(1)} reshape(bf16[64,6,1536]{2,1,0:T(8,128)(2,1)} %all_to_all.10) | data formatting | bytes 2359296 | tf_op jit(solution)/shard_map/reshape | solution.py:179
  137.7 1.7 fusion.16
  139.5 0.4 convolution_convert_fusion.1
  140.0 0.7 copy.51
  140.7 45.9 %all_to_all.11 = bf16[64,6,1536]{2,1,0:T(8,128)(2,1)S(1)} all-to-all(bf16[64,6,1536]{2,1,0:T(8,128)(2,1)S(1)} %copy.51), channel_id=1, replica_groups=mesh['rep'=2,'req'=32,'tp'=4] {'rep','req'}, dimensions={0} | all-to-all | bytes 2359296 | tf_op jit(solution)/shard_map/all_to_all | solution.py:187
  186.6 1.2 reshape.206
  187.8 1.8 convolution_convert_fusion.2
  189.6 0.9 copy.54
  190.6 19.2 %reduce-scatter.4.cloned.1.call-done = bf16[384,16]{1,0:T(8,128)(2,1)} async-done(((bf16[1536,16]{1,0:T(8,128)(2,1)}), bf16[384,16]{1,0:T(8,128)(2,1)}) %reduce-scatter.4.cloned.1.call-update) | async-done | bytes 12304
  209.7 1.0 copy.55
  210.7 0.6 add_convert_fusion.1
  (66 shorter events, 2.8 us)
Async XLA Ops:
  6.5 57.9 %copy-start = (bf16[384,1536]{1,0:T(8,128)(2,1)S(1)}, bf16[384,1536]{1,0:T(8,128)(2,1)}, u32[]{:S(2)}) copy-start(bf16[384,1536]{1,0:T(8,128)(2,1)} %param.21) | copy-start | bytes 3538948
  6.5 203.2 %reduce-scatter.4.cloned.1.call-start = ((), (), s32[]{:S(2)}) async-start(), calls=%async_computation.3 | async-start | bytes 491520
  14.8 22.5 %collective-permute-start = (bf16[1,262528]{1,0:T(2,128)(2,1)}, bf16[1,262528]{1,0:T(2,128)(2,1)S(1)}, u32[]{:S(2)}, u32[]{:S(2)}) collective-permute-start(bf16[1,262528]{1,0:T(2,128)(2,1)} %pad_maximum_fusion), channel_id=1, source_target_pairs={{0,128},{128,0},{1,129},{129,1},{2,130},{130,2},{3,131},{131,3},{4... | collective-permute-start | bytes 1575176 | tf_op jit(solution)/shard_map/ppermute | solution.py:13
  14.8 21.2 %copy-start.6 = (s32[16,8]{0,1:T(8,128)S(1)}, s32[16,8]{0,1:T(8,128)}, u32[]{:S(2)}) copy-start(s32[16,8]{0,1:T(8,128)} %param.24) | copy-start | bytes 1540
  14.8 21.9 %copy-start.7 = (f32[16,8]{0,1:T(8,128)S(1)}, f32[16,8]{0,1:T(8,128)}, u32[]{:S(2)}) copy-start(f32[16,8]{0,1:T(8,128)} %param.25) | copy-start | bytes 1540
  14.8 22.2 %copy-start.8 = (s32[2,16]{1,0:T(2,128)S(1)}, s32[2,16]{1,0:T(2,128)}, u32[]{:S(2)}) copy-start(s32[2,16]{1,0:T(2,128)} %param.14) | copy-start | bytes 388
  37.3 13.4 %collective-permute-start.1 = (bf16[16,384]{1,0:T(8,128)(2,1)S(1)}, bf16[16,384]{1,0:T(8,128)(2,1)S(1)}, u32[]{:S(2)}, u32[]{:S(2)}) collective-permute-start(bf16[16,384]{1,0:T(8,128)(2,1)S(1)} %dynamic_update_slice.18), channel_id=1, source_target_pairs={{0,1},{1,2},{2,3},{3,0},{4,5},{5,6},{6,7},{7,4},{8,9},{9,10},{10,1... | collective-permute-start | bytes 36872 | tf_op jit(solution)/shard_map/ppermute | solution.py:48
  38.9 12.4 %collective-permute-start.2 = (bf16[16,384]{1,0:T(8,128)(2,1)S(1)}, bf16[16,384]{1,0:T(8,128)(2,1)S(1)}, u32[]{:S(2)}, u32[]{:S(2)}) collective-permute-start(bf16[16,384]{1,0:T(8,128)(2,1)S(1)} %dynamic_update_slice.18), channel_id=1, source_target_pairs={{0,3},{1,0},{2,1},{3,2},{4,7},{5,4},{6,5},{7,6},{8,11},{9,8},{10,9... | collective-permute-start | bytes 36872 | tf_op jit(solution)/shard_map/ppermute | solution.py:53
  49.4 6.7 %copy-start.1 = (bf16[1536,384]{1,0:T(8,128)(2,1)S(1)}, bf16[1536,384]{1,0:T(8,128)(2,1)}, u32[]{:S(2)}) copy-start(bf16[1536,384]{1,0:T(8,128)(2,1)} %param.19) | copy-start | bytes 3538948
  49.4 6.6 %copy-start.4 = (f32[1536]{0:T(1024)S(1)}, f32[1536]{0:T(1024)}, u32[]{:S(2)}) copy-start(f32[1536]{0:T(1024)} %param.17) | copy-start | bytes 18436
  50.7 5.8 %copy-start.2 = (bf16[1536,256]{1,0:T(8,128)(2,1)S(1)}, bf16[1536,256]{1,0:T(8,128)(2,1)}, u32[]{:S(2)}) copy-start(bf16[1536,256]{1,0:T(8,128)(2,1)} %param.20) | copy-start | bytes 2359300
  50.8 5.2 %collective-permute-start.3 = (bf16[16,384]{1,0:T(8,128)(2,1)S(1)}, bf16[16,384]{1,0:T(8,128)(2,1)S(1)}, u32[]{:S(2)}, u32[]{:S(2)}) collective-permute-start(bf16[16,384]{1,0:T(8,128)(2,1)S(1)} %collective-permute-done.1), channel_id=1, source_target_pairs={{0,1},{1,2},{2,3},{3,0},{4,5},{5,6},{6,7},{7,4},{8,9},{9,10},{10,1... | collective-permute-start | bytes 36872 | tf_op jit(solution)/shard_map/ppermute | solution.py:48
  64.3 15.5 %copy-start.5 = (f32[1536]{0:T(1024)S(1)}, f32[1536]{0:T(1024)}, u32[]{:S(2)}) copy-start(f32[1536]{0:T(1024)} %param.18) | copy-start | bytes 18436
  137.7 1.8 copy-start.3
Sparse Core Ops, SparseCore 0:
  190.7 18.9 reduce-scatter.3
